TPU v7x, 32 devices: a whole 2x2x4 slice. The times are simulated.
32 devices in a mesh: lat: 4 (over y, x), lon: 8 (over z, core).
Axes of the slice: x: 2, y: 2, z: 4, core: 2. Of those that a mesh axis runs over, the one named last changes fastest.
Arguments:
- grid_state: float32 [48, 120, 384], P('lat', 'lon'), may hold values from -6 to 6
- norm_gain: float32 [2, 384], replicated, may hold values from 0.25 to 1.75
- conv_weight: bfloat16 [2, 3, 3, 384, 384], replicated, may hold values from -0.109375 to 0.109375
- filter_weight: bfloat16 [48, 384, 384], P('lat'), may hold values from -0.3125 to 0.3125
- degree_keep: int32 [48, 48], P('lat', 'lon'), may hold values 0 or 1
Outputs:
- updated: float32 [48, 120, 384], P('lat', 'lon')
Inputs may be any that keep to these rules, and one draw needn't show every extreme that they name: degree_keep[l, m] is 0 or 1 for degree l and order m.
All inputs are finite; a program needn't handle non-finite values. No bound on the sum of `degree_keep` on one device may be relied on, other than what follows from the above.
Results may differ from a plain program's by a relative error of at most 0.008.
Values may be sent and summed in bfloat16 or wider, within the bound.
A program may use at most 64 MiB of HBM per device.

v0:
```python
import math
import jax
import jax.numpy as jnp
from jax import lax
from jax.sharding import PartitionSpec as P

epsilon = 1e-06


def extended(array, sides, width):
    for axis, dim in sides:
        size, length = (lax.axis_size(axis), array.shape[dim])
        up = [(i, (i + 1) % size) for i in range(size)]
        down = [(j, i) for i, j in up]
        last = lax.slice_in_dim(array, length - width, length, axis=dim)
        first = lax.slice_in_dim(array, 0, width, axis=dim)
        before = lax.ppermute(last, axis, up)
        after = lax.ppermute(first, axis, down)
        array = jnp.concatenate([before, array, after], axis=dim)
    return array


def colatitude(row_index, total_rows, float_type):
    theta_rows = (row_index.astype(float_type) + 0.5) * (math.pi / total_rows)
    return (jnp.cos(theta_rows), jnp.sin(theta_rows))


def legendre_table(orders, cosine, sine_values, amount):
    float_type = cosine.dtype
    order_f = orders.astype(float_type)[:, None]
    order_i = orders[:, None]
    column = cosine[None, :]
    log_start = (
        0.5
        * (
            jnp.log((2.0 * order_f + 1.0) / (4.0 * math.pi))
            + jax.scipy.special.gammaln(order_f + 0.5)
            - jax.scipy.special.gammaln(order_f + 1.0)
            - 0.5 * math.log(math.pi)
        )
        + order_f * jnp.log(sine_values)[None, :]
    )
    sectoral = jnp.exp(log_start)

    def advance(carry, degree):
        before, latest = carry
        degree_f = degree.astype(float_type)
        growth = jnp.sqrt(
            jnp.maximum(4.0 * degree_f * degree_f - 1.0, 1.0)
            / jnp.maximum(degree_f * degree_f - order_f * order_f, 1.0)
        )
        prior = degree_f - 1.0
        damping = jnp.sqrt(
            jnp.maximum(prior * prior - order_f * order_f, 0.0)
            / jnp.maximum(4.0 * prior * prior - 1.0, 1.0)
        )
        grown = growth * (column * latest - damping * before)
        fresh = jnp.where(
            degree < order_i, jnp.zeros_like(grown), jnp.where(degree == order_i, sectoral, grown)
        )
        return ((latest, fresh), fresh)

    zero_rows = jnp.zeros((orders.shape[0], cosine.shape[0]), float_type)
    _, assoc_basis = lax.scan(
        advance, (zero_rows, zero_rows), jnp.arange(amount, dtype=jnp.int32), unroll=16
    )
    return assoc_basis


def forward_table(columns, modes, total_cols, float_type):
    lon_index = columns[:, None]
    order_index = jnp.arange(modes, dtype=jnp.int32)[None, :]
    phase = (lon_index * order_index % total_cols).astype(float_type) * (2.0 * math.pi / total_cols)
    factor = 2.0 * math.pi / total_cols
    return jnp.stack([jnp.cos(phase) * factor, -jnp.sin(phase) * factor], axis=2).reshape(
        columns.shape[0], 2 * modes
    )


def inverse_table(modes, total_cols, float_type):
    order_index = jnp.arange(modes, dtype=jnp.int32)[:, None]
    lon_index = jnp.arange(total_cols, dtype=jnp.int32)[None, :]
    phase = (lon_index * order_index % total_cols).astype(float_type) * (2.0 * math.pi / total_cols)
    factor = jnp.where(order_index == 0, 1.0, 2.0).astype(float_type)
    return jnp.stack([jnp.cos(phase) * factor, -jnp.sin(phase) * factor], axis=1).reshape(
        2 * modes, total_cols
    )


def paired(form, data, table):
    upper_part = table.astype(jnp.bfloat16)
    lower_part = (table - upper_part.astype(jnp.float32)).astype(jnp.bfloat16)
    first = jnp.einsum(form, data, upper_part, preferred_element_type=jnp.float32)
    return first + jnp.einsum(form, data, lower_part, preferred_element_type=jnp.float32)


def to_columns(values):
    return lax.all_to_all(values, "lon", split_axis=2, concat_axis=0, tiled=True)


def to_channels(values):
    return lax.all_to_all(values, "lon", split_axis=0, concat_axis=2, tiled=True)


def grid_rims(normed):
    padded = extended(normed, (("lat", 0), ("lon", 1)), 1)
    place = lax.axis_index("lat")
    final_place = lax.axis_size("lat") - 1
    zero_line = jnp.zeros_like(padded[:1])
    upper_rim = jnp.where(place == 0, zero_line, padded[:1])
    lower_rim = jnp.where(place == final_place, zero_line, padded[-1:])
    return jnp.concatenate([upper_rim, padded[1:-1], lower_rim], axis=0)


def conv_taps(padded, weight, row_count, col_count):
    channels = padded.shape[2]
    running = jnp.zeros((row_count * col_count, weight.shape[3]), jnp.float32)
    for row_tap in range(3):
        for col_tap in range(3):
            window = padded[row_tap : row_tap + row_count, col_tap : col_tap + col_count].reshape(
                row_count * col_count, channels
            )
            running = running + jnp.dot(
                window, weight[row_tap, col_tap], preferred_element_type=jnp.float32
            )
    return running.reshape(row_count, col_count, weight.shape[3])


def conv_block(grid_state, gain, weight):
    row_count, col_count, channels = grid_state.shape
    scale_rows = lax.rsqrt(jnp.mean(grid_state * grid_state, axis=-1, keepdims=True) + epsilon)
    normed = (grid_state * scale_rows * gain).astype(jnp.bfloat16)
    padded = grid_rims(normed)
    mixture = conv_taps(padded, weight, row_count, col_count)
    return grid_state + jax.nn.gelu(mixture, approximate=False)


def per_device(grid_state, norm_gain, conv_weight, filter_weight, degree_keep):
    f32 = jnp.float32
    for depth_index in range(2):
        grid_state = conv_block(grid_state, norm_gain[depth_index], conv_weight[depth_index])
    row_count, col_count, channels = grid_state.shape
    lat_parts = lax.axis_size("lat")
    lon_parts = lax.axis_size("lon")
    total_rows = row_count * lat_parts
    total_cols = col_count * lon_parts
    local_modes = total_rows // lon_parts
    share = channels // lon_parts
    columns = to_columns(jnp.transpose(grid_state.astype(jnp.bfloat16), (1, 0, 2)))
    flat_columns = columns.reshape(total_cols, row_count * share)
    dft_table = forward_table(jnp.arange(total_cols), total_rows, total_cols, f32)
    spectrum = paired("lx,lk->kx", flat_columns, dft_table).astype(jnp.bfloat16)
    spectrum = to_channels(spectrum.reshape(2 * total_rows, row_count, share))
    spectrum = jnp.transpose(spectrum, (1, 0, 2)).reshape(row_count, local_modes, 2 * channels)
    orders = lax.axis_index("lon") * local_modes + jnp.arange(local_modes, dtype=jnp.int32)
    keep_mask = degree_keep.astype(f32)
    cosine, sine_values = colatitude(jnp.arange(total_rows), total_rows, f32)
    assoc_basis = legendre_table(orders, cosine, sine_values, total_rows)
    weighted = assoc_basis * (sine_values * (math.pi / total_rows))[None, None, :]
    first_here = lax.axis_index("lat") * row_count
    own_weighted = lax.dynamic_slice_in_dim(weighted, first_here, row_count, 0)
    own_rows_basis = lax.dynamic_slice_in_dim(assoc_basis, first_here, row_count, 2)
    basis_rows = own_weighted
    coefficients = paired(
        "imx,lmi->lmx", lax.all_gather(spectrum, "lat", axis=0, tiled=True), basis_rows
    ).astype(jnp.bfloat16)
    flat_coeffs = coefficients.reshape(row_count, 2 * local_modes, channels)
    mixture = jnp.einsum("lkc,lcd->lkd", flat_coeffs, filter_weight, preferred_element_type=f32)
    mixture = mixture.reshape(row_count, local_modes, 2, channels) * keep_mask[:, :, None, None]
    filtered = mixture.reshape(row_count, local_modes, 2 * channels).astype(jnp.bfloat16)
    basis_rows = own_rows_basis
    synthesis = paired(
        "lmx,lmi->imx", lax.all_gather(filtered, "lat", axis=0, tiled=True), basis_rows
    ).astype(jnp.bfloat16)
    by_order = jnp.transpose(synthesis.reshape(row_count, 2 * local_modes, channels), (1, 0, 2))
    returned = to_columns(by_order)
    flat_returned = returned.reshape(2 * total_rows, row_count * share)
    physical = paired(
        "kx,kl->lx", flat_returned, inverse_table(total_rows, total_cols, f32)
    ).astype(jnp.bfloat16)
    physical = to_channels(physical.reshape(total_cols, row_count, share))
    physical = jnp.transpose(physical, (1, 0, 2))
    return grid_state + jax.nn.gelu(physical.astype(f32), approximate=False)


def solution(mesh):
    in_specs = (P("lat", "lon", None), P(), P(), P("lat", None, None), P("lat", "lon"))
    out_specs = P("lat", "lon", None)
    return jax.shard_map(
        per_device, mesh=mesh, in_specs=in_specs, out_specs=out_specs, check_vma=False
    )
```

profile of v0, /device:TPU:0, one launch (start us, length us, event | category | flops | bytes accessed | tf_op | source)
XLA Modules:
  0.0 426.2 jit_solution(8437420346642597354)
XLA Ops:
  4.9 3.0 collective-permute-start
  11.8 5.6 %slice_bitcast_fusion = (bf16[3,3,384,384]{3,2,1,0:T(8,128)(2,1)}, bf16[3,3,384,384]{3,2,1,0:T(8,128)(2,1)}) fusion(bf16[2,3,3,384,384]{4,3,2,1,0:T(8,128)(2,1)} %param.9), kind=kLoop, calls=%fused_computation.125 | loop fusion | bytes 10616832 | tf_op jit(solution)/shard_map/squeeze | solution.py:141
  17.4 152.1 %while.21 = (s32[]{:T(128)}, f32[6,48]{1,0:T(8,128)}, f32[6,48]{1,0:T(8,128)}, f32[3,16,6,48]{3,2,1,0:T(8,128)}, s32[3,16]{1,0:T(4,128)}, /*index=5*/s32[]{:T(12...) while((s32[]{:T(128)}, f32[6,48]{1,0:T(8,128)}, ...), condition=%wide.region_3.4_spmd.clone.clone.clone.clone, body=%wide.region_2.3_spmd.clone.clone.clone.clone.sunk | while | flops 65138 | bytes 363896 | solution.py:64
  169.5 2.0 fusion.72
  174.8 3.5 collective-permute-start.3
  184.7 2.0 fusion.73
  195.0 2.0 fusion.71
  208.5 2.0 negate_multiply_fusion.1
  224.2 3.5 collective-permute-start.7
  227.7 2.0 fusion.69
  238.2 2.0 fusion.70
  246.7 2.0 fusion.68
  258.6 2.0 negate_multiply_fusion
  264.1 2.5 convert_bitcast_fusion
  266.6 2.8 copy.96
  269.4 3.5 reshape.1588
  272.9 4.0 all-to-all-start
  283.8 3.5 reshape.1589
  287.3 3.4 copy.97
  290.6 2.1 reshape.1569
  297.3 2.0 copy.100
  299.2 2.1 reshape.1590
  301.3 4.3 %all-to-all-start.1 = ((bf16[8,2,3456]{2,1,0:T(2,128)(2,1)}), bf16[8,2,3456]{2,1,0:T(2,128)(2,1)}, u32[]{:S(2)}, u32[]{:S(2)}) async-start(bf16[8,2,3456]{2,1,0:T(2,128)(2,1)} %reshape.1590), calls=%async_computation.1 | async-start | bytes 221184 | tf_op jit(solution)/shard_map/all_to_all | solution.py:102
  306.4 5.8 %all-to-all-done.1 = bf16[8,2,3456]{2,1,0:T(2,128)(2,1)} async-done(((bf16[8,2,3456]{2,1,0:T(2,128)(2,1)}), bf16[8,2,3456]{2,1,0:T(2,128)(2,1)}, u32[]{:S(2)}, u32[]{:S(2)}) %all-to-all-start.1) | async-done | bytes 110624 | tf_op jit(solution)/shard_map/all_to_all | solution.py:102
  312.2 2.1 reshape.1591
  321.4 11.5 %all_gather.6 = bf16[48,6,768]{2,1,0:T(8,128)(2,1)S(1)} all-gather(bf16[12,6,768]{2,1,0:T(8,128)(2,1)} %reshape.1571), channel_id=1, replica_groups=mesh['lat'=4,'lon'=8] {'lat'}, dimensions={0}, use_global_device_ids=true | all-gather | bytes 552960 | tf_op jit(solution)/shard_map/all_gather | solution.py:165
  337.4 2.2 fusion.151
  342.4 10.4 %all_gather.7 = bf16[48,6,768]{2,1,0:T(8,128)(2,1)S(1)} all-gather(bf16[12,6,768]{2,1,0:T(8,128)(2,1)S(1)} %multiply_convert_fusion), channel_id=1, replica_groups=mesh['lat'=4,'lon'=8] {'lat'}, dimensions={0}, use_global_device_ids=true | all-gather | bytes 552960 | tf_op jit(solution)/shard_map/all_gather | solution.py:173
  357.2 2.8 copy.111
  360.0 3.4 reshape.1592
  363.4 4.0 all-to-all-start.2
  370.2 3.7 all-to-all-done.2
  373.9 3.4 reshape.1593
  377.3 3.2 copy.112
  385.5 2.1 copy.114
  387.6 2.2 reshape.1594
  389.8 10.8 %all_to_all.57 = bf16[8,2,4320]{2,1,0:T(2,128)(2,1)} all-to-all(bf16[8,2,4320]{2,1,0:T(2,128)(2,1)} %reshape.1594), channel_id=1, replica_groups=mesh['lat'=4,'lon'=8] {'lon'}, dimensions={0} | all-to-all | bytes 276480 | tf_op jit(solution)/shard_map/all_to_all | solution.py:102
  400.6 2.2 reshape.1595
  402.9 2.0 copy.115
  406.6 2.1 copy.116
  408.7 2.1 reshape.1579
  410.8 2.2 copy.117
  413.0 2.1 mul.1989
  415.2 2.1 copy.118
  417.3 2.1 reshape.1582
  419.3 2.2 copy.119
  421.6 2.1 mul.1992
  423.7 2.5 fusion.67
  (444 shorter events, 241.2 us)
Async XLA Ops:
  0.0 337.4 %copy-start = (bf16[12,384,384]{2,1,0:T(8,128)(2,1)S(1)}, bf16[12,384,384]{2,1,0:T(8,128)(2,1)}, u32[]{:S(2)}) copy-start(bf16[12,384,384]{2,1,0:T(8,128)(2,1)} %param.10) | copy-start | bytes 10616836
  4.9 168.3 %collective-permute-start = (bf16[1,15,384]{2,1,0:T(8,128)(2,1)}, bf16[1,15,384]{2,1,0:T(8,128)(2,1)}, u32[]{:S(2)}, u32[]{:S(2)}) collective-permute-start(bf16[1,15,384]{2,1,0:T(8,128)(2,1)} %get-tuple-element.566), channel_id=1, source_target_pairs={{0,8},{8,16},{16,24},{24,0},{1,9},{9,17},{17,25},{25,1},{2,10},{10... | collective-permute-start | bytes 34568 | tf_op jit(solution)/shard_map/ppermute | solution.py:17
  7.8 165.4 %collective-permute-start.1 = (bf16[1,15,384]{2,1,0:T(8,128)(2,1)}, bf16[1,15,384]{2,1,0:T(8,128)(2,1)}, u32[]{:S(2)}, u32[]{:S(2)}) collective-permute-start(bf16[1,15,384]{2,1,0:T(8,128)(2,1)} %get-tuple-element.567), channel_id=1, source_target_pairs={{8,0},{16,8},{24,16},{0,24},{9,1},{17,9},{25,17},{1,25},{10,2},{18... | collective-permute-start | bytes 34568 | tf_op jit(solution)/shard_map/ppermute | solution.py:18
  21.4 3.8 copy-start.3
  30.6 4.2 copy-start.22
  31.2 3.5 copy-start.20
  31.2 3.5 copy-start.21
  42.2 6.6 %copy-start.25 = (f32[6]{0:T(128)}, f32[6]{0:T(128)S(1)}, u32[]{:S(2)}) copy-start(f32[6]{0:T(128)S(1)} %get-tuple-element.771) | copy-start | bytes 76 | tf_op jit(solution)/shard_map/while
  42.8 3.4 copy-start.30
  42.8 3.4 copy-start.31
  50.2 4.5 %copy-start.6 = (f32[6,48]{1,0:T(8,128)}, f32[6,48]{1,0:T(8,128)S(1)}, u32[]{:S(2)}) copy-start(f32[6,48]{1,0:T(8,128)S(1)} %get-tuple-element.790) | copy-start | bytes 3460 | tf_op jit(solution)/shard_map/while
  64.0 4.1 copy-start.18
  72.1 3.8 copy-start.3
  81.3 4.2 copy-start.22
  81.9 3.5 copy-start.20
  81.9 3.5 copy-start.21
  92.9 6.6 %copy-start.25 = (f32[6]{0:T(128)}, f32[6]{0:T(128)S(1)}, u32[]{:S(2)}) copy-start(f32[6]{0:T(128)S(1)} %get-tuple-element.771) | copy-start | bytes 76 | tf_op jit(solution)/shard_map/while
  93.5 3.4 copy-start.30
  93.5 3.4 copy-start.31
  100.9 4.5 %copy-start.6 = (f32[6,48]{1,0:T(8,128)}, f32[6,48]{1,0:T(8,128)S(1)}, u32[]{:S(2)}) copy-start(f32[6,48]{1,0:T(8,128)S(1)} %get-tuple-element.790) | copy-start | bytes 3460 | tf_op jit(solution)/shard_map/while
  114.6 4.1 copy-start.18
  122.8 3.8 copy-start.3
  132.0 4.2 copy-start.22
  132.6 3.5 copy-start.20
  132.6 3.5 copy-start.21
  143.6 6.6 %copy-start.25 = (f32[6]{0:T(128)}, f32[6]{0:T(128)S(1)}, u32[]{:S(2)}) copy-start(f32[6]{0:T(128)S(1)} %get-tuple-element.771) | copy-start | bytes 76 | tf_op jit(solution)/shard_map/while
  144.2 3.4 copy-start.30
  151.6 4.5 %copy-start.6 = (f32[6,48]{1,0:T(8,128)}, f32[6,48]{1,0:T(8,128)S(1)}, u32[]{:S(2)}) copy-start(f32[6,48]{1,0:T(8,128)S(1)} %get-tuple-element.790) | copy-start | bytes 3460 | tf_op jit(solution)/shard_map/while
  165.3 4.1 copy-start.18
  174.8 5.3 %collective-permute-start.2 = (bf16[14,1,384]{2,1,0:T(2,128)(2,1)}, bf16[14,1,384]{2,1,0:T(2,128)(2,1)}, u32[]{:S(2)}, u32[]{:S(2)}) collective-permute-start(bf16[14,1,384]{2,1,0:T(2,128)(2,1)} %get-tuple-element.560), channel_id=1, source_target_pairs={{0,1},{1,2},{2,3},{3,4},{4,5},{5,6},{6,7},{7,0},{8,9},{9,10},{10,1... | collective-permute-start | bytes 32264 | tf_op jit(solution)/shard_map/ppermute | solution.py:17
  174.8 5.3 %collective-permute-start.3 = (bf16[14,1,384]{2,1,0:T(2,128)(2,1)}, bf16[14,1,384]{2,1,0:T(2,128)(2,1)}, u32[]{:S(2)}, u32[]{:S(2)}) collective-permute-start(bf16[14,1,384]{2,1,0:T(2,128)(2,1)} %get-tuple-element.561), channel_id=1, source_target_pairs={{1,0},{2,1},{3,2},{4,3},{5,4},{6,5},{7,6},{0,7},{9,8},{10,9},{11,1... | collective-permute-start | bytes 32264 | tf_op jit(solution)/shard_map/ppermute | solution.py:18
  201.9 4.1 copy-start.7
  201.9 4.1 copy-start.12
  201.9 5.4 %copy-start.13 = (bf16[180,384]{1,0:T(8,128)(2,1)S(1)}, bf16[180,384]{1,0:T(8,128)(2,1)}, u32[]{:S(2)}) copy-start(bf16[180,384]{1,0:T(8,128)(2,1)} %reshape.1554) | copy-start | bytes 414724
  201.9 6.6 %copy-start.9 = (bf16[180,384]{1,0:T(8,128)(2,1)S(1)}, bf16[180,384]{1,0:T(8,128)(2,1)}, u32[]{:S(2)}) copy-start(bf16[180,384]{1,0:T(8,128)(2,1)} %reshape.1555) | copy-start | bytes 414724
  206.1 9.8 %copy-start.38 = (f32[384]{0:T(512)S(1)}, f32[384]{0:T(512)}, u32[]{:S(2)}) copy-start(f32[384]{0:T(512)} %get-tuple-element.402) | copy-start | bytes 4612
  217.2 5.9 %collective-permute-start.4 = (bf16[1,15,384]{2,1,0:T(8,128)(2,1)}, bf16[1,15,384]{2,1,0:T(8,128)(2,1)S(1)}, u32[]{:S(2)}, u32[]{:S(2)}) collective-permute-start(bf16[1,15,384]{2,1,0:T(8,128)(2,1)} %get-tuple-element.564), channel_id=1, source_target_pairs={{0,8},{8,16},{16,24},{24,0},{1,9},{9,17},{17,25},{25,1},{2,10},{10... | collective-permute-start | bytes 34568 | tf_op jit(solution)/shard_map/ppermute | solution.py:17
  218.3 4.8 %collective-permute-start.5 = (bf16[1,15,384]{2,1,0:T(8,128)(2,1)}, bf16[1,15,384]{2,1,0:T(8,128)(2,1)}, u32[]{:S(2)}, u32[]{:S(2)}) collective-permute-start(bf16[1,15,384]{2,1,0:T(8,128)(2,1)} %get-tuple-element.565), channel_id=1, source_target_pairs={{8,0},{16,8},{24,16},{0,24},{9,1},{17,9},{25,17},{1,25},{10,2},{18... | collective-permute-start | bytes 34568 | tf_op jit(solution)/shard_map/ppermute | solution.py:18
  224.1 5.6 %collective-permute-start.6 = (bf16[14,1,384]{2,1,0:T(2,128)(2,1)S(1)}, bf16[14,1,384]{2,1,0:T(2,128)(2,1)S(1)}, u32[]{:S(2)}, u32[]{:S(2)}) collective-permute-start(bf16[14,1,384]{2,1,0:T(2,128)(2,1)S(1)} %get-tuple-element.556), channel_id=1, source_target_pairs={{0,1},{1,2},{2,3},{3,4},{4,5},{5,6},{6,7},{7,0},{8,9},{9,10},{10,1... | collective-permute-start | bytes 32264 | tf_op jit(solution)/shard_map/ppermute | solution.py:17
  224.2 5.5 %collective-permute-start.7 = (bf16[14,1,384]{2,1,0:T(2,128)(2,1)S(1)}, bf16[14,1,384]{2,1,0:T(2,128)(2,1)S(1)}, u32[]{:S(2)}, u32[]{:S(2)}) collective-permute-start(bf16[14,1,384]{2,1,0:T(2,128)(2,1)S(1)} %get-tuple-element.557), channel_id=1, source_target_pairs={{1,0},{2,1},{3,2},{4,3},{5,4},{6,5},{7,6},{0,7},{9,8},{10,9},{11,1... | collective-permute-start | bytes 32264 | tf_op jit(solution)/shard_map/ppermute | solution.py:18
  252.0 4.1 copy-start.8
  252.0 4.1 copy-start.11
  252.0 5.4 %copy-start.14 = (bf16[180,384]{1,0:T(8,128)(2,1)S(1)}, bf16[180,384]{1,0:T(8,128)(2,1)}, u32[]{:S(2)}) copy-start(bf16[180,384]{1,0:T(8,128)(2,1)} %reshape.1563) | copy-start | bytes 414724
  252.0 6.6 %copy-start.10 = (bf16[180,384]{1,0:T(8,128)(2,1)S(1)}, bf16[180,384]{1,0:T(8,128)(2,1)}, u32[]{:S(2)}) copy-start(bf16[180,384]{1,0:T(8,128)(2,1)} %reshape.1564) | copy-start | bytes 414724
  264.1 17.1 %copy-start.39 = (s32[12,6]{0,1:T(8,128)S(1)}, s32[12,6]{0,1:T(8,128)}, u32[]{:S(2)}) copy-start(s32[12,6]{0,1:T(8,128)} %param.11) | copy-start | bytes 868
  272.9 10.9 %all-to-all-start = ((bf16[8,2,4320]{2,1,0:T(2,128)(2,1)}), bf16[8,2,4320]{2,1,0:T(2,128)(2,1)}, u32[]{:S(2)}, u32[]{:S(2)}) async-start(bf16[8,2,4320]{2,1,0:T(2,128)(2,1)} %reshape.1588), calls=%async_computation | async-start | bytes 278528 | tf_op jit(solution)/shard_map/all_to_all | solution.py:98
  301.3 10.9 %all-to-all-start.1 = ((bf16[8,2,3456]{2,1,0:T(2,128)(2,1)}), bf16[8,2,3456]{2,1,0:T(2,128)(2,1)}, u32[]{:S(2)}, u32[]{:S(2)}) async-start(bf16[8,2,3456]{2,1,0:T(2,128)(2,1)} %reshape.1590), calls=%async_computation.1 | async-start | bytes 221184 | tf_op jit(solution)/shard_map/all_to_all | solution.py:102
  363.4 10.5 %all-to-all-start.2 = ((bf16[8,2,3456]{2,1,0:T(2,128)(2,1)}), bf16[8,2,3456]{2,1,0:T(2,128)(2,1)}, u32[]{:S(2)}, u32[]{:S(2)}) async-start(bf16[8,2,3456]{2,1,0:T(2,128)(2,1)} %reshape.1592), calls=%async_computation.2 | async-start | bytes 221184 | tf_op jit(solution)/shard_map/all_to_all | solution.py:98
  (51 other events, 108.1 us)
where the time goes:
time: 432 us; the launch traced here: 426 us
  other arithmetic  142 us (33%)
  local copies, waits for them, and re-layouts  140 us (32%)
  matrix products  41.5 us (10%)
  blocking collectives  32.7 us (8%)
  loops' own time  31.1 us (7%)
  starting transfers between devices  26.3 us (6%)
  waiting for transfers between devices  11.3 us (3%)
    while x45, other arithmetic  62.3 us
    eq x48, other arithmetic, advance(): degree == order_i  31.6 us
    another operation x1, loops' own time, legendre_table(): lax.scan(advance, (zero_rows, zero_rows), jnp.arange(amount, dtype=jnp.in...  31.1 us
    dot_general x18, matrix products, conv_taps(): jnp.dot(window, weight[row_tap, col_tap], preferred_element_type=jnp.floa...  29.2 us
    reshape x18, local copies, waits for them, and re-layouts, conv_taps(): padded[row_tap:row_tap + row_count, col_tap:col_tap + col_count]  29.2 us
    unnamed x41, local copies, waits for them, and re-layouts  26.1 us
    mul x8, local copies, waits for them, and re-layouts, per_device(): return grid_state + jax.nn.gelu(physical.astype(f32), approximate=False)  17.1 us
    sqrt x27, other arithmetic, advance(): jnp.sqrt(jnp.maximum(prior * prior - order_f * order_f, 0.0) / jnp.maximu...  13.6 us
  transfers between devices with their start and end apart: 11, of which 4 were waited for; matrix products, arithmetic and copies ran while one was open for 35% of the time, Pallas kernels for 0%

commit v1 on v0

--- a/solution.py
+++ b/solution.py
@@ -5,6 +5,12 @@
 from jax.sharding import PartitionSpec as P
 
 epsilon = 1e-06
+
+
+def exchange_blocks(array, axis, split, join):
+    shards = jnp.split(array, lax.axis_size(axis), axis=split)
+    arrived = lax.all_to_all(jnp.stack(shards), axis, 0, 0)
+    return jnp.concatenate(arrived, axis=join)
 
 
 def extended(array, sides, width):
@@ -99,7 +105,7 @@
 
 
 def to_channels(values):
-    return lax.all_to_all(values, "lon", split_axis=0, concat_axis=2, tiled=True)
+    return exchange_blocks(values, "lon", 0, 2)
 
 
 def grid_rims(normed):

time: 432 us -> 478 us (1.11)
  local copies, waits for them, and re-layouts: 140 us -> 200 us
  matrix products: 41.5 us -> 25.8 us
    another operation x0 -> x18, local copies, waits for them, and re-layouts: none -> 27.8 us  [exchange_blocks(): arrived = lax.all_to_all(jnp.stack(shards), axis, 0, 0)]
    unnamed x41 -> x77, local copies, waits for them, and re-layouts: 26.1 us -> 51.1 us
    slice x0 -> x15, local copies, waits for them, and re-layouts: none -> 19.5 us  [the longest x12 17.5 us: conv_taps(): padded[row_tap:row_tap + row_count, col_tap:col_tap + col_count]]
    dot_general x18, matrix products: 29.2 us -> 14.8 us  [conv_taps(): jnp.dot(window, weight[row_tap, col_tap], preferred_element_type=jnp.floa...]
    mul x8 -> x4, local copies, waits for them, and re-layouts: 17.1 us -> 7.97 us  [per_device(): return grid_state + jax.nn.gelu(physical.astype(f32), approximate=False)]
    all_to_all x3 -> x0, local copies, waits for them, and re-layouts: 5.84 us -> none  [to_channels(): lax.all_to_all(values, 'lon', split_axis=0, concat_axis=2, tiled=True)]
  transfers between devices with their start and end apart: 11 -> 11, of which waited for: 4 -> 6; matrix products, arithmetic and copies ran while one was open for 35% -> 31% of each run, Pallas kernels for 0% -> 0%
where the time goes in v1:
time: 478 us; the launch traced here: 471 us
  local copies, waits for them, and re-layouts  200 us (42%)
  other arithmetic  140 us (29%)
  blocking collectives  32.8 us (7%)
  loops' own time  31.8 us (7%)
  starting transfers between devices  26.8 us (6%)
  matrix products  25.8 us (5%)
  waiting for transfers between devices  12.9 us (3%)
    while x45, other arithmetic  62.2 us
    unnamed x77, local copies, waits for them, and re-layouts  51.1 us
    eq x48, other arithmetic, advance(): degree == order_i  32.3 us
    another operation x1, loops' own time, legendre_table(): lax.scan(advance, (zero_rows, zero_rows), jnp.arange(amount, dtype=jnp.in...  31.8 us
    reshape x18, local copies, waits for them, and re-layouts, conv_taps(): padded[row_tap:row_tap + row_count, col_tap:col_tap + col_count]  29.1 us
    another operation x18, local copies, waits for them, and re-layouts, exchange_blocks(): arrived = lax.all_to_all(jnp.stack(shards), axis, 0, 0)  27.8 us
    slice x12, local copies, waits for them, and re-layouts, conv_taps(): padded[row_tap:row_tap + row_count, col_tap:col_tap + col_count]  17.5 us
    dot_general x18, matrix products, conv_taps(): jnp.dot(window, weight[row_tap, col_tap], preferred_element_type=jnp.floa...  14.8 us
  transfers between devices with their start and end apart: 11, of which 6 were waited for; matrix products, arithmetic and copies ran while one was open for 31% of the time, Pallas kernels for 0%

profile of v1, /device:TPU:0, one launch (start us, length us, event | category | flops | bytes accessed | tf_op | source)
XLA Modules:
  0.0 470.6 jit_solution(1066870435012493100)
XLA Ops:
  4.9 3.0 collective-permute-start
  10.1 153.6 %while.21 = (s32[]{:T(128)}, f32[6,48]{1,0:T(8,128)}, f32[6,48]{1,0:T(8,128)}, f32[3,16,6,48]{3,2,1,0:T(8,128)}, s32[3,16]{1,0:T(4,128)}, /*index=5*/s32[]{:T(12...) while((s32[]{:T(128)}, f32[6,48]{1,0:T(8,128)}, ...), condition=%wide.region_3.4_spmd.clone.clone.clone.clone, body=%wide.region_2.3_spmd.clone.clone.clone.clone.sunk | while | flops 65138 | bytes 363896 | solution.py:70
  163.7 5.6 %slice_bitcast_fusion = (bf16[3,3,384,384]{3,2,1,0:T(8,128)(2,1)}, bf16[3,3,384,384]{3,2,1,0:T(8,128)(2,1)}) fusion(bf16[2,3,3,384,384]{4,3,2,1,0:T(8,128)(2,1)} %param.9), kind=kLoop, calls=%fused_computation.125 | loop fusion | bytes 10616832 | tf_op jit(solution)/shard_map/squeeze | solution.py:147
  172.2 1.7 constant_dynamic-slice_fusion.1
  176.2 3.5 collective-permute-start.3
  192.5 1.8 pad_maximum_fusion.12
  214.9 1.7 mul.1943
  216.6 1.7 mul.1945
  218.3 1.8 multiply_reduce_fusion
  222.1 1.9 collective-permute-start.5
  231.2 3.5 collective-permute-start.7
  238.6 1.8 pad_maximum_fusion.6
  242.1 3.0 pad_maximum_fusion
  272.6 1.7 mul.1954
  274.3 1.7 mul.1956
  276.1 2.5 convert_bitcast_fusion
  278.6 2.9 copy.389
  281.5 3.5 reshape.1616
  284.9 4.5 all-to-all-start
  296.4 3.5 reshape.1617
  299.9 3.4 copy.390
  303.3 2.0 reshape.1603
  331.2 2.1 reshape.1618
  333.2 4.4 all-to-all-start.1
  338.4 5.8 %all-to-all-done.1 = bf16[8,2,3456]{2,1,0:T(2,128)(2,1)} async-done(((bf16[8,2,3456]{2,1,0:T(2,128)(2,1)}), bf16[8,2,3456]{2,1,0:T(2,128)(2,1)}, u32[]{:S(2)}, u32[]{:S(2)}) %all-to-all-start.1) | async-done | bytes 110624 | tf_op jit(solution)/shard_map/all_to_all | solution.py:12
  344.2 2.1 reshape.1619
  346.3 1.9 copy.392
  348.2 1.9 reshape.1605
  353.3 11.6 %all_gather.6 = bf16[48,6,768]{2,1,0:T(8,128)(2,1)S(1)} all-gather(bf16[12,6,768]{2,1,0:T(8,128)(2,1)} %reshape.1606), channel_id=1, replica_groups=mesh['lat'=4,'lon'=8] {'lat'}, dimensions={0}, use_global_device_ids=true | all-gather | bytes 552960 | tf_op jit(solution)/shard_map/all_gather | solution.py:171
  369.4 2.3 fusion.149
  371.7 1.7 reshape.1608
  374.5 10.4 %all_gather.7 = bf16[48,6,768]{2,1,0:T(8,128)(2,1)S(1)} all-gather(bf16[12,6,768]{2,1,0:T(8,128)(2,1)S(1)} %multiply_convert_fusion), channel_id=1, replica_groups=mesh['lat'=4,'lon'=8] {'lat'}, dimensions={0}, use_global_device_ids=true | all-gather | bytes 552960 | tf_op jit(solution)/shard_map/all_gather | solution.py:179
  389.3 2.8 copy.401
  392.1 3.4 reshape.1620
  395.5 4.0 all-to-all-start.2
  402.2 3.7 all-to-all-done.2
  406.0 3.4 reshape.1621
  409.4 3.3 copy.402
  412.6 2.0 reshape.1610
  418.2 1.7 copy.404
  443.0 2.1 reshape.1622
  445.2 10.8 %all_to_all.40 = bf16[8,2,4320]{2,1,0:T(2,128)(2,1)} all-to-all(bf16[8,2,4320]{2,1,0:T(2,128)(2,1)} %reshape.1622), channel_id=1, replica_groups=mesh['lat'=4,'lon'=8] {'lon'}, dimensions={0} | all-to-all | bytes 276480 | tf_op jit(solution)/shard_map/all_to_all | solution.py:12
  456.0 2.2 reshape.1623
  458.2 2.0 fusion.48
  461.5 2.1 mul.1989
  463.6 2.4 copy.413
  466.0 2.1 mul.1992
  468.2 2.5 fusion.65
  (512 shorter events, 286.7 us)
Async XLA Ops:
  0.0 369.4 %copy-start = (bf16[12,384,384]{2,1,0:T(8,128)(2,1)S(1)}, bf16[12,384,384]{2,1,0:T(8,128)(2,1)}, u32[]{:S(2)}) copy-start(bf16[12,384,384]{2,1,0:T(8,128)(2,1)} %param.10) | copy-start | bytes 10616836
  4.9 164.4 %collective-permute-start = (bf16[1,15,384]{2,1,0:T(8,128)(2,1)}, bf16[1,15,384]{2,1,0:T(8,128)(2,1)}, u32[]{:S(2)}, u32[]{:S(2)}) collective-permute-start(bf16[1,15,384]{2,1,0:T(8,128)(2,1)} %get-tuple-element.574), channel_id=1, source_target_pairs={{0,8},{8,16},{16,24},{24,0},{1,9},{9,17},{17,25},{25,1},{2,10},{10... | collective-permute-start | bytes 34568 | tf_op jit(solution)/shard_map/ppermute | solution.py:23
  7.8 161.4 %collective-permute-start.1 = (bf16[1,15,384]{2,1,0:T(8,128)(2,1)}, bf16[1,15,384]{2,1,0:T(8,128)(2,1)}, u32[]{:S(2)}, u32[]{:S(2)}) collective-permute-start(bf16[1,15,384]{2,1,0:T(8,128)(2,1)} %get-tuple-element.575), channel_id=1, source_target_pairs={{8,0},{16,8},{24,16},{0,24},{9,1},{17,9},{25,17},{1,25},{10,2},{18... | collective-permute-start | bytes 34568 | tf_op jit(solution)/shard_map/ppermute | solution.py:24
  14.0 4.0 copy-start.3
  23.2 4.1 copy-start.30
  23.9 3.5 copy-start.26
  23.9 3.5 copy-start.27
  35.2 6.6 %copy-start.33 = (f32[6]{0:T(128)}, f32[6]{0:T(128)S(1)}, u32[]{:S(2)}) copy-start(f32[6]{0:T(128)S(1)} %get-tuple-element.787) | copy-start | bytes 76 | tf_op jit(solution)/shard_map/while
  43.1 4.6 copy-start.8
  57.0 4.3 copy-start.24
  65.2 4.0 copy-start.3
  74.4 4.1 copy-start.30
  75.1 3.5 copy-start.26
  75.1 3.5 copy-start.27
  86.4 6.6 %copy-start.33 = (f32[6]{0:T(128)}, f32[6]{0:T(128)S(1)}, u32[]{:S(2)}) copy-start(f32[6]{0:T(128)S(1)} %get-tuple-element.787) | copy-start | bytes 76 | tf_op jit(solution)/shard_map/while
  87.0 3.4 copy-start.38
  94.4 4.6 copy-start.8
  108.2 4.3 copy-start.24
  116.4 4.0 copy-start.3
  125.6 4.1 copy-start.30
  126.3 3.5 copy-start.26
  126.3 3.5 copy-start.27
  137.6 6.6 %copy-start.33 = (f32[6]{0:T(128)}, f32[6]{0:T(128)S(1)}, u32[]{:S(2)}) copy-start(f32[6]{0:T(128)S(1)} %get-tuple-element.787) | copy-start | bytes 76 | tf_op jit(solution)/shard_map/while
  145.6 4.6 copy-start.8
  159.4 4.3 copy-start.24
  172.2 7.6 %collective-permute-start.2 = (bf16[14,1,384]{2,0,1:T(8,128)(2,1)}, bf16[14,1,384]{2,0,1:T(8,128)(2,1)S(1)}, u32[]{:S(2)}, u32[]{:S(2)}) collective-permute-start(bf16[14,1,384]{2,0,1:T(8,128)(2,1)} %copy.426), channel_id=1, source_target_pairs={{0,1},{1,2},{2,3},{3,4},{4,5},{5,6},{6,7},{7,0},{8,9},{9,10},{10,1... | collective-permute-start | bytes 32264 | tf_op jit(solution)/shard_map/ppermute | solution.py:23
  176.2 4.9 %collective-permute-start.3 = (bf16[14,1,384]{2,0,1:T(8,128)(2,1)S(1)}, bf16[14,1,384]{2,0,1:T(8,128)(2,1)S(1)}, u32[]{:S(2)}, u32[]{:S(2)}) collective-permute-start(bf16[14,1,384]{2,0,1:T(8,128)(2,1)S(1)} %copy.427), channel_id=1, source_target_pairs={{1,0},{2,1},{3,2},{4,3},{5,4},{6,5},{7,6},{0,7},{9,8},{10,9},{11,1... | collective-permute-start | bytes 32264 | tf_op jit(solution)/shard_map/ppermute | solution.py:24
  207.3 4.1 copy-start.2
  207.3 5.3 %copy-start.13 = (bf16[180,384]{1,0:T(8,128)(2,1)S(1)}, bf16[180,384]{1,0:T(8,128)(2,1)}, u32[]{:S(2)}) copy-start(bf16[180,384]{1,0:T(8,128)(2,1)} %reshape.1585) | copy-start | bytes 414724
  207.3 5.6 %copy-start.16 = (bf16[180,384]{1,0:T(8,128)(2,1)S(1)}, bf16[180,384]{1,0:T(8,128)(2,1)}, u32[]{:S(2)}) copy-start(bf16[180,384]{1,0:T(8,128)(2,1)} %reshape.1586) | copy-start | bytes 414724
  208.8 4.4 copy-start.18
  210.1 3.4 copy-start.20
  213.2 7.6 %copy-start.46 = (f32[384]{0:T(512)S(1)}, f32[384]{0:T(512)}, u32[]{:S(2)}) copy-start(f32[384]{0:T(512)} %get-tuple-element.402) | copy-start | bytes 4612
  221.0 5.3 %copy-start.6 = (bf16[12,15,384]{2,1,0:T(8,128)(2,1)}, bf16[12,15,384]{2,1,0:T(8,128)(2,1)S(1)}, u32[]{:S(2)}) copy-start(bf16[12,15,384]{2,1,0:T(8,128)(2,1)S(1)} %multiply_convert_fusion.1) | copy-start | bytes 414724
  221.0 4.6 collective-permute-start.4
  222.1 4.2 collective-permute-start.5
  224.1 4.2 copy-start.28
  224.1 4.2 copy-start.29
  228.3 6.5 %collective-permute-start.6 = (bf16[14,1,384]{2,0,1:T(8,128)(2,1)}, bf16[14,1,384]{2,0,1:T(8,128)(2,1)}, u32[]{:S(2)}, u32[]{:S(2)}) collective-permute-start(bf16[14,1,384]{2,0,1:T(8,128)(2,1)} %copy.374), channel_id=1, source_target_pairs={{0,1},{1,2},{2,3},{3,4},{4,5},{5,6},{6,7},{7,0},{8,9},{9,10},{10,1... | collective-permute-start | bytes 32264 | tf_op jit(solution)/shard_map/ppermute | solution.py:23
  231.2 5.2 %collective-permute-start.7 = (bf16[14,1,384]{2,0,1:T(8,128)(2,1)S(1)}, bf16[14,1,384]{2,0,1:T(8,128)(2,1)S(1)}, u32[]{:S(2)}, u32[]{:S(2)}) collective-permute-start(bf16[14,1,384]{2,0,1:T(8,128)(2,1)S(1)} %copy.375), channel_id=1, source_target_pairs={{1,0},{2,1},{3,2},{4,3},{5,4},{6,5},{7,6},{0,7},{9,8},{10,9},{11,1... | collective-permute-start | bytes 32264 | tf_op jit(solution)/shard_map/ppermute | solution.py:24
  265.1 4.1 copy-start.1
  265.1 5.3 %copy-start.14 = (bf16[180,384]{1,0:T(8,128)(2,1)S(1)}, bf16[180,384]{1,0:T(8,128)(2,1)}, u32[]{:S(2)}) copy-start(bf16[180,384]{1,0:T(8,128)(2,1)} %reshape.1594) | copy-start | bytes 414724
  265.1 5.6 %copy-start.15 = (bf16[180,384]{1,0:T(8,128)(2,1)S(1)}, bf16[180,384]{1,0:T(8,128)(2,1)}, u32[]{:S(2)}) copy-start(bf16[180,384]{1,0:T(8,128)(2,1)} %reshape.1595) | copy-start | bytes 414724
  266.6 4.4 copy-start.17
  276.1 17.7 %copy-start.47 = (s32[12,6]{0,1:T(8,128)S(1)}, s32[12,6]{0,1:T(8,128)}, u32[]{:S(2)}) copy-start(s32[12,6]{0,1:T(8,128)} %param.11) | copy-start | bytes 868
  284.9 11.5 %all-to-all-start = ((bf16[8,2,4320]{2,1,0:T(2,128)(2,1)}), bf16[8,2,4320]{2,1,0:T(2,128)(2,1)}, u32[]{:S(2)}, u32[]{:S(2)}) async-start(bf16[8,2,4320]{2,1,0:T(2,128)(2,1)} %reshape.1616), calls=%async_computation | async-start | bytes 278528 | tf_op jit(solution)/shard_map/all_to_all | solution.py:104
  333.2 10.9 %all-to-all-start.1 = ((bf16[8,2,3456]{2,1,0:T(2,128)(2,1)}), bf16[8,2,3456]{2,1,0:T(2,128)(2,1)}, u32[]{:S(2)}, u32[]{:S(2)}) async-start(bf16[8,2,3456]{2,1,0:T(2,128)(2,1)} %reshape.1618), calls=%async_computation.1 | async-start | bytes 221184 | tf_op jit(solution)/shard_map/all_to_all | solution.py:12
  395.5 10.5 %all-to-all-start.2 = ((bf16[8,2,3456]{2,1,0:T(2,128)(2,1)}), bf16[8,2,3456]{2,1,0:T(2,128)(2,1)}, u32[]{:S(2)}, u32[]{:S(2)}) async-start(bf16[8,2,3456]{2,1,0:T(2,128)(2,1)} %reshape.1620), calls=%async_computation.2 | async-start | bytes 221184 | tf_op jit(solution)/shard_map/all_to_all | solution.py:104
  (59 other events, 129.8 us)
